TPU v7x, 32 devices: a whole 2x2x4 slice. The times are simulated.
32 devices in a mesh: gx: 2 (over x), gz: 4 (over y, core), ta: 4 (over z).
Axes of the slice: x: 2, y: 2, z: 4, core: 2. Of those that a mesh axis runs over, the one named last changes fastest.
Arguments:
- velocity: bfloat16 [3, 32, 64, 4096], P(None, 'ta', 'gx', 'gz'), may hold values from -6 to 6
- offsets: int32 [7], replicated, may hold values from 0 to 16, as said below
- owner: int32 [7], replicated, may hold values from 0 to 7, as said below
Outputs:
- cross_spectra: float32 [4, 2, 7, 64, 4096], P(None, None, None, 'gx', ('gz', 'ta'))
Inputs may be any that keep to these rules, and one draw needn't show every extreme that they name: `offsets`: each segment of 16 snapshots lies inside the window. owner o names the block of streamwise index o // 4 and spanwise index o mod 4.
All inputs are finite; a program needn't handle non-finite values.
Results may differ from a plain program's by a relative error of at most 0.0062.
Values may be sent and summed in bfloat16 or wider, within the bound.
No kernel may reach another device: no remote copies, remote signals or barrier semaphores. Data moves between devices by JAX's collectives and lax.ppermute only.
A program may use at most 64 MiB of HBM per device.

v0:
```python
import math
import jax
import jax.numpy as jnp
from jax import lax
from jax.sharding import PartitionSpec as P

SEG = 16
NSEG = 7
F = 7


def from_root(shard, axis, root):
    mine = lax.axis_index(axis) == root
    return lax.psum(jnp.where(mine, shard, jnp.zeros_like(shard)), axis)


def padded_2(shard, sides, width):
    for axis, dim in sides:
        devices, length = (lax.axis_size(axis), shard.shape[dim])
        up = [(i, (i + 1) % devices) for i in range(devices)]
        down = [(j, i) for i, j in up]
        last = lax.slice_in_dim(shard, length - width, length, axis=dim)
        first = lax.slice_in_dim(shard, 0, width, axis=dim)
        before = lax.ppermute(last, axis, up)
        after = lax.ppermute(first, axis, down)
        shard = jnp.concatenate([before, shard, after], axis=dim)
    return shard


def dft_table(offsets, step_count_total):
    sample_times = jnp.arange(step_count_total, dtype=jnp.int32)
    temporal_delay = sample_times[None, :] - offsets[:, None]
    inside = (temporal_delay >= 0) & (temporal_delay < SEG)
    window = 0.5 - 0.5 * jnp.cos(2.0 * math.pi / SEG * temporal_delay.astype(jnp.float32))
    frequency = jnp.arange(1, F + 1, dtype=jnp.int32)
    turns = frequency[None, :, None] * temporal_delay[:, None, :] % SEG
    phase_angle = 2.0 * math.pi / SEG * turns.astype(jnp.float32)
    weight = jnp.where(inside, window, jnp.float32(0.0))[:, None, :]
    rows = jnp.stack([weight * jnp.cos(phase_angle), -weight * jnp.sin(phase_angle)], axis=1)
    return rows.reshape(offsets.shape[0] * 2 * F, step_count_total).astype(jnp.bfloat16)


def fourth_order(padded, which_axis, length_cells):

    def shifted(first):
        return lax.slice_in_dim(padded, first, first + length_cells, axis=which_axis)

    return (8.0 * (shifted(3) - shifted(1)) - (shifted(4) - shifted(0))) / 12.0


def spread_series(block_data, root_index):
    return from_root(block_data, ("gx", "gz"), root_index)


def shards(velocity, offsets, owner):
    block_rows = velocity.shape[2]
    block_cols = velocity.shape[3]
    stream_span = jnp.stack([velocity[0], velocity[2]])
    padded = padded_2(stream_span, (("gx", 2), ("gz", 3)), 2).astype(jnp.float32)
    streamwise = padded[0, :, 2 : 2 + block_rows, :]
    spanwise = padded[1, :, :, 2 : 2 + block_cols]
    vorticity = (
        fourth_order(streamwise, 2, block_cols) - fourth_order(spanwise, 1, block_rows)
    ).astype(jnp.bfloat16)
    fields = jnp.concatenate([velocity, vorticity[None]], axis=0)
    step_count_total = velocity.shape[1] * lax.axis_size("ta")
    segment_rows = dft_table(offsets, step_count_total)
    series = lax.all_to_all(fields, "ta", split_axis=3, concat_axis=1, tiled=True)
    flat_series = series.reshape(series.shape[0], series.shape[1], -1)
    power_spectra = jnp.einsum(
        "rt,qtn->qrn", segment_rows, flat_series, preferred_element_type=jnp.float32
    )
    flat_series, power_spectra = (flat_series, power_spectra)
    quantities = flat_series.shape[0]
    cells_here = flat_series.shape[2]
    slab_cols = cells_here // block_rows
    window_rows = dft_table(jnp.zeros((1,), jnp.int32), SEG)
    cospectrum = jnp.zeros((quantities, F, cells_here), jnp.float32)
    quadrature_spectrum = jnp.zeros((quantities, F, cells_here), jnp.float32)
    for segment in range(NSEG):
        local_spec = power_spectra[:, segment * 2 * F : (segment + 1) * 2 * F, :]
        window_piece = lax.dynamic_slice_in_dim(flat_series, offsets[segment], SEG, 1)
        arrived = spread_series(window_piece, owner[segment])
        remote = jnp.einsum("rt,qtn->qrn", window_rows, arrived, preferred_element_type=jnp.float32)
        remote_cos = remote[:, :F]
        remote_sin = remote[:, F:]
        cosine_part_here = local_spec[:, :F]
        local_sin = local_spec[:, F:]
        cospectrum = cospectrum + (remote_cos * cosine_part_here + remote_sin * local_sin)
        quadrature_spectrum = quadrature_spectrum + (
            remote_cos * local_sin - remote_sin * cosine_part_here
        )
    scaling = 8.0 / (3.0 * SEG * NSEG)
    result = jnp.stack([cospectrum, quadrature_spectrum], axis=1) * scaling
    return result.reshape(quantities, 2, F, block_rows, slab_cols)


def solution(mesh):
    in_specs = (P(None, "ta", "gx", "gz"), P(), P())
    out_specs = P(None, None, None, "gx", ("gz", "ta"))
    return jax.shard_map(shards, mesh=mesh, in_specs=in_specs, out_specs=out_specs, check_vma=False)
```

profile of v0, /device:TPU:0, one launch (start us, length us, event | category | flops | bytes accessed | tf_op | source)
XLA Modules:
  0.0 293.2 jit_solution(14867775583435725023)
XLA Ops:
  6.5 1.3 fusion.28
  8.1 3.0 %collective-permute-start = (bf16[2,8,2,1024]{3,1,2,0:T(8,128)(2,1)S(1)}, bf16[2,8,2,1024]{3,1,2,0:T(8,128)(2,1)S(1)}, u32[]{:S(2)}, u32[]{:S(2)}) collective-permute-start(bf16[2,8,2,1024]{3,1,2,0:T(8,128)(2,1)S(1)} %copy.47), channel_id=1, source_target_pairs={{0,16},{16,0},{1,17},{17,1},{2,18},{18,2},{3,19},{19,3},{4,20},{20... | collective-permute-start | bytes 196616 | tf_op jit(solution)/shard_map/ppermute | solution.py:24
  11.2 2.2 collective-permute-done
  14.0 1.5 collective-permute-done.1
  15.7 1.7 collective-permute-start.3
  17.4 6.1 %copy.34 = bf16[3,8,32,1024]{2,1,0,3:T(8,128)(2,1)} copy(bf16[3,8,32,1024]{3,2,1,0:T(8,128)(2,1)S(1)} %copy-done) | data formatting | bytes 3145728 | tf_op args[0]
  23.5 1.4 concatenate.11
  24.8 4.7 %copy.33 = bf16[2,8,36,1028]{2,1,3,0:T(8,128)(2,1)} copy(bf16[2,8,36,1028]{3,1,2,0:T(8,128)(2,1)S(1)} %concatenate.11) | data formatting | bytes 2368512 | tf_op jit(solution)/shard_map/concatenate | solution.py:26
  29.5 2.5 convert_element_type.78
  32.4 1.2 slice_bitcast_fusion
  33.6 4.4 %fusion.8 = bf16[1,8,32,1024]{2,1,0,3:T(8,128)(2,1)} fusion(f32[8,36,1024]{1,0,2:T(8,128)S(1)} %slice_bitcast_fusion.1, f32[8,32,1028]{1,0,2:T(8,128)S(1)} %slice_bitcast_fusion), kind=kLoop, calls=%fused_computation.23 | loop fusion | flops 3145728 | bytes 8912896 | tf_op jit(solution)/shard_map/broadcast_in_dim | solution.py:65
  38.1 6.7 %fusion.33 = bf16[1024,4,8,32]{3,2,1,0:T(8,128)(2,1)} fusion(bf16[1,8,32,1024]{2,1,0,3:T(8,128)(2,1)} %fusion.8, bf16[3,8,32,1024]{2,1,0,3:T(8,128)(2,1)S(1)} %bitcast.65), kind=kLoop, calls=%fused_computation.82 | loop fusion | flops 1048576 | bytes 4194304
  44.8 10.6 %reshape.340 = bf16[4,2,131072]{2,1,0:T(2,128)(2,1)} reshape(bf16[1024,4,8,32]{3,2,1,0:T(8,128)(2,1)} %fusion.33) | data formatting | bytes 4194304
  55.4 5.0 %all-to-all-start = ((bf16[4,2,131072]{2,1,0:T(2,128)(2,1)}), bf16[4,2,131072]{2,1,0:T(2,128)(2,1)S(1)}, u32[]{:S(2)}, u32[]{:S(2)}) async-start(bf16[4,2,131072]{2,1,0:T(2,128)(2,1)} %reshape.340), calls=%async_computation | async-start | bytes 4194304 | tf_op jit(solution)/shard_map/all_to_all | solution.py:68
  60.4 0.7 fusion.32
  69.8 0.7 fusion.31
  79.1 29.5 %all-to-all-done = bf16[4,2,131072]{2,1,0:T(2,128)(2,1)S(1)} async-done(((bf16[4,2,131072]{2,1,0:T(2,128)(2,1)}), bf16[4,2,131072]{2,1,0:T(2,128)(2,1)S(1)}, u32[]{:S(2)}, u32[]{:S(2)}) %all-to-all-start) | async-done | bytes 2097184 | tf_op jit(solution)/shard_map/all_to_all | solution.py:68
  108.6 5.6 %reshape.341 = bf16[1024,4,8,32]{3,2,1,0:T(8,128)(2,1)} reshape(bf16[4,2,131072]{2,1,0:T(2,128)(2,1)S(1)} %all-to-all-done) | data formatting | bytes 4194304
  114.3 8.8 %copy.35 = bf16[4,8,32,4,256]{4,1,2,3,0:T(8,128)(2,1)S(1)} copy(bf16[4,8,32,4,256]{2,1,0,4,3:T(8,128)(2,1)} %bitcast.63) | data formatting | bytes 4194304 | tf_op jit(solution)/shard_map/all_to_all | solution.py:68
  123.1 4.5 %dynamic-slice_select_fusion.6 = (bf16[4,16,8192]{2,1,0:T(8,128)(2,1)}, bf16[4,16,8192]{2,1,0:T(8,128)(2,1)}, bf16[4,16,8192]{2,1,0:T(8,128)(2,1)}, bf16[4,16,81...) fusion(bf16[4,32,8192]{2,1,0:T(8,128)(2,1)S(1)} %bitcast.61, ...), kind=kLoop, calls=%fused_computation.35 | loop fusion | flops 3670016 | bytes 14680099 | tf_op jit(solution)/shard_map/jit(_where)/select_n | solution.py:14
  128.3 7.6 %convolution_bitcast_fusion = f32[4,98,8192]{2,1,0:T(8,128)} fusion(bf16[4,32,8192]{2,1,0:T(8,128)(2,1)S(1)} %bitcast.62, bf16[98,32]{1,0:T(8,128)(2,1)S(1)} %convert_element_type.85), kind=kOutput, calls=%fused_computation | convolution fusion | flops 205520896 | bytes 14948480 | tf_op jit(solution)/shard_map/rt,qtn->qrn/dot_general | solution.py:70
  135.9 105.2 %all-reduce.3.cloned.1.call-done = (bf16[4,16,8192]{2,1,0:T(8,128)(2,1)}, bf16[4,16,8192]{2,1,0:T(8,128)(2,1)}, bf16[4,16,8192]{2,1,0:T(8,128)(2,1)}, bf16[4,16,...) async-done(((bf16[4,16,8192]{2,1,0:T(8,128)(2,1)}, bf16[4,16,8192]{2,1,0:T(8,128)(2,1)}, ...) | async-done | bytes 7340048 | tf_op jit(solution)/shard_map/psum | solution.py:14
  241.1 1.7 convolution_bitcast_fusion.1
  243.3 0.8 copy-done.6
  244.6 1.7 convolution_bitcast_fusion.4
  246.3 1.7 convolution_bitcast_fusion.5
  248.1 1.7 convolution_bitcast_fusion.6
  249.8 1.8 convolution_bitcast_fusion.7
  251.6 15.3 %subtract_add_fusion = f32[4,7,8192]{2,1,0:T(8,128)} fusion(f32[4,98,8192]{2,1,0:T(8,128)} %convolution_bitcast_fusion, f32[4,14,8192]{2,1,0:T(8,128)S(1)} %convolution_bitcast_fusion.1, f32[4,14,8192]{2,1,0:T(8,128)S(1)} %convolution_bitcast_fusion.2, f32[4,14,8192]{2,1,0:T(8,128)S(1)} %convolution_bitcast_fusion.3, ...), kind=kLoop, calls=%fused_computation.27 | loop fusion | flops 6193152 | bytes 26607616 | tf_op jit(solution)/shard_map/add | solution.py:90
  266.9 15.6 %add_add_fusion = f32[4,7,8192]{2,1,0:T(8,128)} fusion(f32[4,98,8192]{2,1,0:T(8,128)} %convolution_bitcast_fusion, f32[4,14,8192]{2,1,0:T(8,128)S(1)} %convolution_bitcast_fusion.1, f32[4,14,8192]{2,1,0:T(8,128)S(1)} %convolution_bitcast_fusion.2, f32[4,14,8192]{2,1,0:T(8,128)S(1)} %convolution_bitcast_fusion.3, ...), kind=kLoop, calls=%fused_computation.28 | loop fusion | flops 6193152 | bytes 26607616 | tf_op jit(solution)/shard_map/add | solution.py:89
  282.6 1.8 reshape.339
  285.1 1.3 copy.39
  (53 shorter events, 3.6 us)
Async XLA Ops:
  7.9 9.5 %copy-start = (bf16[3,8,32,1024]{3,2,1,0:T(8,128)(2,1)S(1)}, bf16[3,8,32,1024]{3,2,1,0:T(8,128)(2,1)}, u32[]{:S(2)}) copy-start(bf16[3,8,32,1024]{3,2,1,0:T(8,128)(2,1)} %param.3) | copy-start | bytes 4718596
  8.1 5.3 %collective-permute-start = (bf16[2,8,2,1024]{3,1,2,0:T(8,128)(2,1)S(1)}, bf16[2,8,2,1024]{3,1,2,0:T(8,128)(2,1)S(1)}, u32[]{:S(2)}, u32[]{:S(2)}) collective-permute-start(bf16[2,8,2,1024]{3,1,2,0:T(8,128)(2,1)S(1)} %copy.47), channel_id=1, source_target_pairs={{0,16},{16,0},{1,17},{17,1},{2,18},{18,2},{3,19},{19,3},{4,20},{20... | collective-permute-start | bytes 196616 | tf_op jit(solution)/shard_map/ppermute | solution.py:24
  11.1 4.3 %collective-permute-start.1 = (bf16[2,8,2,1024]{3,1,2,0:T(8,128)(2,1)S(1)}, bf16[2,8,2,1024]{3,1,2,0:T(8,128)(2,1)S(1)}, u32[]{:S(2)}, u32[]{:S(2)}) collective-permute-start(bf16[2,8,2,1024]{3,1,2,0:T(8,128)(2,1)S(1)} %copy.48), channel_id=1, source_target_pairs={{16,0},{0,16},{17,1},{1,17},{18,2},{2,18},{19,3},{3,19},{20,4},{4,... | collective-permute-start | bytes 196616 | tf_op jit(solution)/shard_map/ppermute | solution.py:25
  15.6 7.9 %collective-permute-start.2 = (bf16[2,8,36,2]{3,1,2,0:T(8,128)(2,1)S(1)}, bf16[2,8,36,2]{3,1,2,0:T(8,128)(2,1)S(1)}, u32[]{:S(2)}, u32[]{:S(2)}) collective-permute-start(bf16[2,8,36,2]{3,1,2,0:T(8,128)(2,1)S(1)} %get-tuple-element.22), channel_id=1, source_target_pairs={{0,4},{4,8},{8,12},{12,0},{1,5},{5,9},{9,13},{13,1},{2,6},{6,10},{... | collective-permute-start | bytes 6920 | tf_op jit(solution)/shard_map/ppermute | solution.py:24
  15.7 7.8 %collective-permute-start.3 = (bf16[2,8,36,2]{3,1,2,0:T(8,128)(2,1)S(1)}, bf16[2,8,36,2]{3,1,2,0:T(8,128)(2,1)S(1)}, u32[]{:S(2)}, u32[]{:S(2)}) collective-permute-start(bf16[2,8,36,2]{3,1,2,0:T(8,128)(2,1)S(1)} %get-tuple-element.21), channel_id=1, source_target_pairs={{4,0},{8,4},{12,8},{0,12},{5,1},{9,5},{13,9},{1,13},{6,2},{10,6},{... | collective-permute-start | bytes 6920 | tf_op jit(solution)/shard_map/ppermute | solution.py:25
  32.3 5.7 %slice-start = ((s8[6291456]{0:T(1024)(128)(4,1)}), s8[4194304]{0:T(1024)(128)(4,1)S(1)}, s32[]{:S(2)}) async-start(s8[6291456]{0:T(1024)(128)(4,1)} %bitcast.64), calls=%async_computation.2 | async-start | bytes 8388608
  33.6 4.5 %slice-start.1 = ((s8[6291456]{0:T(1024)(128)(4,1)}), s8[2097152]{0:T(1024)(128)(4,1)S(1)}, s32[]{:S(2)}) async-start(s8[6291456]{0:T(1024)(128)(4,1)} %bitcast.64), calls=%async_computation.3 | async-start | bytes 4194304
  55.4 5.0 %copy-start.8 = (s32[7]{0:T(128)S(1)}, s32[7]{0:T(128)}, u32[]{:S(2)}) copy-start(s32[7]{0:T(128)} %param.4) | copy-start | bytes 88
  55.4 14.4 %copy-start.9 = (s32[7]{0:T(128)S(1)}, s32[7]{0:T(128)}, u32[]{:S(2)}) copy-start(s32[7]{0:T(128)} %param.5) | copy-start | bytes 88
  55.4 53.3 %all-to-all-start = ((bf16[4,2,131072]{2,1,0:T(2,128)(2,1)}), bf16[4,2,131072]{2,1,0:T(2,128)(2,1)S(1)}, u32[]{:S(2)}, u32[]{:S(2)}) async-start(bf16[4,2,131072]{2,1,0:T(2,128)(2,1)} %reshape.340), calls=%async_computation | async-start | bytes 4194304 | tf_op jit(solution)/shard_map/all_to_all | solution.py:68
  60.4 180.7 %all-reduce.3.cloned.1.call-start = ((), (), s32[]{:S(2)}) async-start(), calls=%async_computation.1 | async-start | bytes 14680064 | tf_op jit(solution)/shard_map/psum | solution.py:14
  241.1 1.7 copy-start.7
  242.9 1.2 copy-start.6
  243.3 1.3 copy-start.5
  244.5 1.8 copy-start.4
  246.3 1.8 copy-start.3
  248.1 1.7 copy-start.2
  282.6 1.8 copy-start.1
Sparse Core Ops, SparseCore 0:
  127.8 113.3 all-reduce.2
where the time goes:
time: 294 us; the launch traced here: 293 us
  waiting for transfers between devices  138 us (47%)
  other arithmetic  50.1 us (17%)
  local copies, waits for them, and re-layouts  46.7 us (16%)
  between operations  31 us (11%)
  matrix products  17.1 us (6%)
  starting transfers between devices  9.91 us (3%)
    psum x1, waiting for transfers between devices, from_root(): return lax.psum(jnp.where(mine, shard, jnp.zeros_like(shard)), axis)  105 us
    all_to_all x1, waiting for transfers between devices, shards(): lax.all_to_all(fields, 'ta', split_axis=3, concat_axis=1, tiled=True)  29.5 us
    unnamed x31, local copies, waits for them, and re-layouts  23.8 us
    add x1, other arithmetic, shards(): cospectrum + (remote_cos * cosine_part_here + remote_sin * local_sin)  15.6 us
    add x1, other arithmetic, shards(): quadrature_spectrum + (remote_cos * local_sin - remote_sin * cosine_part_...  15.3 us
    dot_general x7, matrix products, shards(): jnp.einsum('rt,qtn->qrn', window_rows, arrived, preferred_element_type=jn...  9.5 us
    all_to_all x1, local copies, waits for them, and re-layouts, shards(): lax.all_to_all(fields, 'ta', split_axis=3, concat_axis=1, tiled=True)  8.82 us
    dot_general x1, matrix products, shards(): jnp.einsum('rt,qtn->qrn', segment_rows, flat_series, preferred_element_ty...  7.59 us
  transfers between devices with their start and end apart: 6, of which 4 were waited for; matrix products, arithmetic and copies ran while one was open for 6% of the time, Pallas kernels for 0%

commit v1 on v0

--- a/solution.py
+++ b/solution.py
@@ -7,6 +7,18 @@
 SEG = 16
 NSEG = 7
 F = 7
+
+
+def pools_carry(v0):
+    return jnp.concatenate(
+        lax.all_to_all(
+            jnp.stack(jnp.split(v0, lax.axis_size("ta"), 3)),
+            concat_axis=0,
+            split_axis=0,
+            axis_name="ta",
+        ),
+        1,
+    )
 
 
 def from_root(shard, axis, root):
@@ -65,7 +77,7 @@
     fields = jnp.concatenate([velocity, vorticity[None]], axis=0)
     step_count_total = velocity.shape[1] * lax.axis_size("ta")
     segment_rows = dft_table(offsets, step_count_total)
-    series = lax.all_to_all(fields, "ta", split_axis=3, concat_axis=1, tiled=True)
+    series = pools_carry(fields)
     flat_series = series.reshape(series.shape[0], series.shape[1], -1)
     power_spectra = jnp.einsum(
         "rt,qtn->qrn", segment_rows, flat_series, preferred_element_type=jnp.float32

time: 294 us -> 257 us (0.87)
  local copies, waits for them, and re-layouts: 46.7 us -> 14.1 us
  other arithmetic: 50.1 us -> 40 us
  waiting for transfers between devices: 138 us -> 144 us
    unnamed x31 -> x22, local copies, waits for them, and re-layouts: 23.8 us -> 2.76 us
    all_to_all x1 -> x0, local copies, waits for them, and re-layouts: 8.82 us -> none  [shards(): lax.all_to_all(fields, 'ta', split_axis=3, concat_axis=1, tiled=True)]
    unnamed x2 -> x0, other arithmetic: 6.74 us -> none
    concatenate x3 -> x1, local copies, waits for them, and re-layouts: 6.07 us -> 1.46 us  [padded_2(): shard = jnp.concatenate([before, shard, after], axis=dim)]
    broadcast_in_dim x1, other arithmetic: 4.44 us -> 0.88 us  [shards(): fields = jnp.concatenate([velocity, vorticity[None]], axis=0)]
    reshape x0 -> x1, local copies, waits for them, and re-layouts: none -> 3.01 us  [pools_carry(): jnp.concatenate(lax.all_to_all(jnp.stack(jnp.split(v0, lax.axis_size('ta'...]
    ppermute x2, starting transfers between devices: 3.09 us -> 0.14 us  [padded_2(): before = lax.ppermute(last, axis, up)]
    ppermute x2, starting transfers between devices: 1.82 us -> 4.76 us  [padded_2(): after = lax.ppermute(first, axis, down)]
  transfers between devices with their start and end apart: 6 -> 6, of which waited for: 4 -> 6; matrix products, arithmetic and copies ran while one was open for 6% -> 4% of each run, Pallas kernels for 0% -> 0%
where the time goes in v1:
time: 257 us
  waiting for transfers between devices  144 us (56%)
  other arithmetic  40 us (16%)
  between operations  31.7 us (12%)
  matrix products  17.3 us (7%)
  local copies, waits for them, and re-layouts  14.1 us (5%)
  starting transfers between devices  9.91 us (4%)
    psum x1, waiting for transfers between devices, from_root(): return lax.psum(jnp.where(mine, shard, jnp.zeros_like(shard)), axis)  106 us
    all_to_all x1, waiting for transfers between devices, pools_carry(): lax.all_to_all(jnp.stack(jnp.split(v0, lax.axis_size('ta'), 3)), concat_a...  29.8 us
    add x1, other arithmetic, shards(): quadrature_spectrum + (remote_cos * local_sin - remote_sin * cosine_part_...  15.5 us
    add x1, other arithmetic, shards(): cospectrum + (remote_cos * cosine_part_here + remote_sin * local_sin)  15.3 us
    dot_general x7, matrix products, shards(): jnp.einsum('rt,qtn->qrn', window_rows, arrived, preferred_element_type=jn...  9.52 us
    dot_general x1, matrix products, shards(): jnp.einsum('rt,qtn->qrn', segment_rows, flat_series, preferred_element_ty...  7.8 us
  transfers between devices with their start and end apart: 6, of which 6 were waited for; matrix products, arithmetic and copies ran while one was open for 4% of the time, Pallas kernels for 0%

profile of v1, /device:TPU:0, one launch (start us, length us, event | category | flops | bytes accessed | tf_op | source)
XLA Modules:
  0.0 256.8 jit_solution(14168843192717132232)
XLA Ops:
  6.5 1.3 fusion.35
  7.9 3.0 %collective-permute-start.1 = (bf16[2,8,2,1024]{3,2,1,0:T(2,128)(2,1)S(1)}, bf16[2,8,2,1024]{3,2,1,0:T(2,128)(2,1)S(1)}, u32[]{:S(2)}, u32[]{:S(2)}) collective-permute-start(bf16[2,8,2,1024]{3,2,1,0:T(2,128)(2,1)S(1)} %get-tuple-element.28), channel_id=1, source_target_pairs={{16,0},{0,16},{17,1},{1,17},{18,2},{2,18},{19,3},{3,19},{20,4},{4,... | collective-permute-start | bytes 196616 | tf_op jit(solution)/shard_map/ppermute | solution.py:37
  11.1 2.3 collective-permute-done.1
  13.3 1.9 collective-permute-done
  15.2 0.7 pad_maximum_fusion.2
  16.2 1.7 collective-permute-start.3
  17.9 3.0 %collective-permute-done.2 = bf16[2,8,36,2]{3,2,1,0:T(8,128)(2,1)S(1)} collective-permute-done((bf16[2,8,36,2]{3,2,1,0:T(8,128)(2,1)S(1)}, bf16[2,8,36,2]{3,2,1,0:T(8,128)(2,1)S(1)}, u32[]{:S(2)}, u32[]{:S(2)}) %collective-permute-start.2) | collective-permute-done | bytes 2336 | tf_op jit(solution)/shard_map/ppermute | solution.py:36
  20.9 0.8 collective-permute-done.3
  21.7 1.5 concatenate.11
  23.9 0.9 fusion.15
  24.8 0.5 copy-done.1
  25.6 1.6 pad_maximum_fusion
  27.2 5.0 %all-to-all-start = ((bf16[4,4,8,32,256]{4,3,2,1,0:T(8,128)(2,1)}), bf16[4,4,8,32,256]{4,3,2,1,0:T(8,128)(2,1)S(1)}, u32[]{:S(2)}, u32[]{:S(2)}) async-start(bf16[4,4,8,32,256]{4,3,2,1,0:T(8,128)(2,1)} %pad_maximum_fusion), calls=%async_computation | async-start | bytes 4194304 | tf_op jit(solution)/shard_map/all_to_all | solution.py:14
  32.2 0.7 fusion.38
  41.9 0.7 fusion.37
  51.7 29.8 %all-to-all-done = bf16[4,4,8,32,256]{4,3,2,1,0:T(8,128)(2,1)S(1)} async-done(((bf16[4,4,8,32,256]{4,3,2,1,0:T(8,128)(2,1)}), bf16[4,4,8,32,256]{4,3,2,1,0:T(8,128)(2,1)S(1)}, u32[]{:S(2)}, u32[]{:S(2)}) %all-to-all-start) | async-done | bytes 2097184 | tf_op jit(solution)/shard_map/all_to_all | solution.py:14
  81.4 1.4 copy-done
  82.8 3.0 %copy.7 = bf16[4,4,8,32,256]{4,2,3,1,0:T(8,128)(2,1)S(1)} copy(bf16[4,4,8,32,256]{4,3,2,0,1:T(8,128)(2,1)} %bitcast.66) | data formatting | bytes 4194304 | tf_op jit(solution)/shard_map/reshape | solution.py:13
  85.8 4.5 %dynamic-slice_select_fusion.6 = (bf16[4,16,8192]{2,1,0:T(8,128)(2,1)}, bf16[4,16,8192]{2,1,0:T(8,128)(2,1)}, bf16[4,16,8192]{2,1,0:T(8,128)(2,1)}, bf16[4,16,81...) fusion(bf16[4,32,8192]{2,1,0:T(8,128)(2,1)S(1)} %bitcast.64, ...), kind=kLoop, calls=%fused_computation.40 | loop fusion | flops 3670016 | bytes 14680099 | tf_op jit(solution)/shard_map/jit(_where)/select_n | solution.py:26
  91.0 7.8 %convolution_bitcast_fusion = f32[4,98,8192]{2,1,0:T(8,128)} fusion(bf16[4,32,8192]{2,1,0:T(8,128)(2,1)S(1)} %bitcast.65, bf16[98,32]{1,0:T(8,128)(2,1)S(1)} %convert_element_type.85), kind=kOutput, calls=%fused_computation | convolution fusion | flops 205520896 | bytes 14948480 | tf_op jit(solution)/shard_map/rt,qtn->qrn/dot_general | solution.py:82
  98.8 106.0 %all-reduce.3.cloned.1.call-done = (bf16[4,16,8192]{2,1,0:T(8,128)(2,1)}, bf16[4,16,8192]{2,1,0:T(8,128)(2,1)}, bf16[4,16,8192]{2,1,0:T(8,128)(2,1)}, bf16[4,16,...) async-done(((bf16[4,16,8192]{2,1,0:T(8,128)(2,1)}, bf16[4,16,8192]{2,1,0:T(8,128)(2,1)}, ...) | async-done | bytes 7340048 | tf_op jit(solution)/shard_map/psum | solution.py:26
  204.8 1.7 convolution_bitcast_fusion.1
  207.0 0.8 copy-done.7
  208.3 1.8 convolution_bitcast_fusion.4
  210.0 1.7 convolution_bitcast_fusion.5
  211.8 1.7 convolution_bitcast_fusion.6
  213.5 1.8 convolution_bitcast_fusion.7
  215.2 15.5 %subtract_add_fusion = f32[4,7,8192]{2,1,0:T(8,128)} fusion(f32[4,98,8192]{2,1,0:T(8,128)} %convolution_bitcast_fusion, f32[4,14,8192]{2,1,0:T(8,128)S(1)} %convolution_bitcast_fusion.1, f32[4,14,8192]{2,1,0:T(8,128)S(1)} %convolution_bitcast_fusion.2, f32[4,14,8192]{2,1,0:T(8,128)S(1)} %convolution_bitcast_fusion.3, ...), kind=kLoop, calls=%fused_computation.32 | loop fusion | flops 6193152 | bytes 26607616 | tf_op jit(solution)/shard_map/add | solution.py:102
  230.8 15.3 %add_add_fusion = f32[4,7,8192]{2,1,0:T(8,128)} fusion(f32[4,98,8192]{2,1,0:T(8,128)} %convolution_bitcast_fusion, f32[4,14,8192]{2,1,0:T(8,128)S(1)} %convolution_bitcast_fusion.1, f32[4,14,8192]{2,1,0:T(8,128)S(1)} %convolution_bitcast_fusion.2, f32[4,14,8192]{2,1,0:T(8,128)S(1)} %convolution_bitcast_fusion.3, ...), kind=kLoop, calls=%fused_computation.33 | loop fusion | flops 6193152 | bytes 26607616 | tf_op jit(solution)/shard_map/add | solution.py:101
  246.1 1.8 reshape.338
  247.9 0.5 reshape.337
  248.6 1.3 copy.11
  (42 shorter events, 3.1 us)
Async XLA Ops:
  7.9 5.4 %collective-permute-start.1 = (bf16[2,8,2,1024]{3,2,1,0:T(2,128)(2,1)S(1)}, bf16[2,8,2,1024]{3,2,1,0:T(2,128)(2,1)S(1)}, u32[]{:S(2)}, u32[]{:S(2)}) collective-permute-start(bf16[2,8,2,1024]{3,2,1,0:T(2,128)(2,1)S(1)} %get-tuple-element.28), channel_id=1, source_target_pairs={{16,0},{0,16},{17,1},{1,17},{18,2},{2,18},{19,3},{3,19},{20,4},{4,... | collective-permute-start | bytes 196616 | tf_op jit(solution)/shard_map/ppermute | solution.py:37
  11.0 4.3 %collective-permute-start = (bf16[2,8,2,1024]{3,2,1,0:T(2,128)(2,1)S(1)}, bf16[2,8,2,1024]{3,2,1,0:T(2,128)(2,1)S(1)}, u32[]{:S(2)}, u32[]{:S(2)}) collective-permute-start(bf16[2,8,2,1024]{3,2,1,0:T(2,128)(2,1)S(1)} %get-tuple-element.27), channel_id=1, source_target_pairs={{0,16},{16,0},{1,17},{17,1},{2,18},{18,2},{3,19},{19,3},{4,20},{20... | collective-permute-start | bytes 196616 | tf_op jit(solution)/shard_map/ppermute | solution.py:36
  16.1 4.8 %collective-permute-start.2 = (bf16[2,8,36,2]{3,2,1,0:T(8,128)(2,1)S(1)}, bf16[2,8,36,2]{3,2,1,0:T(8,128)(2,1)S(1)}, u32[]{:S(2)}, u32[]{:S(2)}) collective-permute-start(bf16[2,8,36,2]{3,2,1,0:T(8,128)(2,1)S(1)} %get-tuple-element.26), channel_id=1, source_target_pairs={{0,4},{4,8},{8,12},{12,0},{1,5},{5,9},{9,13},{13,1},{2,6},{6,10},{... | collective-permute-start | bytes 6920 | tf_op jit(solution)/shard_map/ppermute | solution.py:36
  16.2 5.5 %collective-permute-start.3 = (bf16[2,8,36,2]{3,2,1,0:T(8,128)(2,1)S(1)}, bf16[2,8,36,2]{3,2,1,0:T(8,128)(2,1)S(1)}, u32[]{:S(2)}, u32[]{:S(2)}) collective-permute-start(bf16[2,8,36,2]{3,2,1,0:T(8,128)(2,1)S(1)} %get-tuple-element.25), channel_id=1, source_target_pairs={{4,0},{8,4},{12,8},{0,12},{5,1},{9,5},{13,9},{1,13},{6,2},{10,6},{... | collective-permute-start | bytes 6920 | tf_op jit(solution)/shard_map/ppermute | solution.py:37
  23.9 1.4 copy-start.1
  27.2 5.0 %copy-start.9 = (s32[7]{0:T(128)S(1)}, s32[7]{0:T(128)}, u32[]{:S(2)}) copy-start(s32[7]{0:T(128)} %param.4) | copy-start | bytes 88
  27.2 14.7 %copy-start.10 = (s32[7]{0:T(128)S(1)}, s32[7]{0:T(128)}, u32[]{:S(2)}) copy-start(s32[7]{0:T(128)} %param.5) | copy-start | bytes 88
  27.2 54.2 %all-to-all-start = ((bf16[4,4,8,32,256]{4,3,2,1,0:T(8,128)(2,1)}), bf16[4,4,8,32,256]{4,3,2,1,0:T(8,128)(2,1)S(1)}, u32[]{:S(2)}, u32[]{:S(2)}) async-start(bf16[4,4,8,32,256]{4,3,2,1,0:T(8,128)(2,1)} %pad_maximum_fusion), calls=%async_computation | async-start | bytes 4194304 | tf_op jit(solution)/shard_map/all_to_all | solution.py:14
  32.2 172.6 %all-reduce.3.cloned.1.call-start = ((), (), s32[]{:S(2)}) async-start(), calls=%async_computation.1 | async-start | bytes 14680064 | tf_op jit(solution)/shard_map/psum | solution.py:26
  81.4 1.4 copy-start
  204.8 1.7 copy-start.8
  206.5 1.2 copy-start.7
  206.9 1.3 copy-start.6
  208.2 1.9 copy-start.5
  210.0 1.7 copy-start.4
  211.8 1.7 copy-start.3
  246.1 1.8 copy-start.2
Sparse Core Ops, SparseCore 0:
  90.4 114.2 all-reduce.2
